TPU v7x, 32 devices: a whole 2x2x4 slice. The times are simulated.
32 devices in a mesh: groups: 2 (over y), vocab: 8 (over z, x), mp: 2 (over core).
Axes of the slice: x: 2, y: 2, z: 4, core: 2. Of those that a mesh axis runs over, the one named last changes fastest.
Arguments:
- gate_pre: bfloat16 [32, 14336], P(('groups', 'vocab'), 'mp'), parts along dimension 0, may hold values from -6 to 6
- up_pre: bfloat16 [32, 14336], P(('groups', 'vocab'), 'mp'), parts along dimension 0, may hold values from -6 to 6
- down_weight: bfloat16 [8192, 14336], P('vocab', 'mp'), may hold values from -0.046875 to 0.046875
- residual: bfloat16 [32, 8192], P(('groups', 'vocab', 'mp')), parts along dimension 0, may hold values from -36 to 36
- norm_gain: bfloat16 [8192], replicated, may hold values from 0.5 to 1.5
- head_weight: bfloat16 [8192, 4032], P('mp', 'vocab')
- targets: int32 [32], P(('groups', 'mp')), parts along dimension 0, may hold values from 0 to 4031
Outputs:
- log_likelihood: float32 [32], P(('groups', 'mp')), parts along dimension 0
There are 2 independent parts, one for each index of `groups`. A program takes and returns all parts, laid end to end along the dimension named above; an argument that names none is the same for every part. Nothing has to cross between parts.
All inputs are finite; a program needn't handle non-finite values.
Results may differ from a plain program's by a relative error of at most 0.0003.
The roundings to bfloat16 on the way count: a program that leaves them out, or rounds other values in their place, can miss the bound.
Values may be sent and summed in bfloat16 or wider, within the bound.
No kernel may reach another device: no remote copies, remote signals or barrier semaphores. Data moves between devices by JAX's collectives and lax.ppermute only.
A program may use at most 64 MiB of HBM per device.

v0:
```python
import jax
import jax.numpy as jnp
from jax import lax
from jax.sharding import PartitionSpec as P

EPSILON = 1e-05


def merged_2(value, axis, combine):
    everything = jax.tree.map(lambda part: lax.all_gather(part, axis), value)
    first = jax.tree.map(lambda part: part[0], everything)

    def turn(k, so_far):
        return combine(so_far, jax.tree.map(lambda part: part[k], everything))

    return lax.fori_loop(1, lax.axis_size(axis), turn, first)


def merge_stats(earlier, follows):
    joint_max = jnp.maximum(earlier[0], follows[0])
    joint_sum = earlier[1] * jnp.exp(earlier[0] - joint_max) + follows[1] * jnp.exp(
        follows[0] - joint_max
    )
    return (joint_max, joint_sum, earlier[2] + follows[2])


def body(gate_pre, up_pre, down_weight, residual, norm_gain, head_weight, targets):
    vocab_count = lax.axis_size("vocab")
    model_count = lax.axis_size("mp")
    model_index = lax.axis_index("mp")
    vocab_index = lax.axis_index("vocab")
    gated_units = (jax.nn.silu(gate_pre.astype(jnp.float32)) * up_pre.astype(jnp.float32)).astype(
        jnp.bfloat16
    )
    down_terms = lax.dot_general(
        lax.all_gather(gated_units, "vocab", axis=0, tiled=True),
        down_weight,
        (((1,), (1,)), ((), ())),
        preferred_element_type=jnp.float32,
    )
    own_rows = residual.shape[0]
    block_cols = down_weight.shape[0]
    grouped = down_terms.reshape(vocab_count, model_count, own_rows, block_cols)
    arrived = lax.all_to_all(
        lax.all_to_all(grouped, "vocab", split_axis=0, concat_axis=3, tiled=True),
        "mp",
        split_axis=1,
        concat_axis=0,
        tiled=True,
    )
    update = jnp.sum(arrived, axis=(0, 1))
    stream = (residual.astype(jnp.float32) + update).astype(jnp.bfloat16)
    stream = lax.optimization_barrier(stream)
    widened = stream.astype(jnp.float32)
    mean_square = jnp.mean(widened * widened, axis=1, keepdims=True)
    normed = (
        widened * lax.rsqrt(mean_square + EPSILON) * norm_gain.astype(jnp.float32)[None, :]
    ).astype(jnp.bfloat16)
    half_width = head_weight.shape[0]
    halves = lax.dynamic_slice_in_dim(
        lax.all_gather(normed, ("vocab", "mp"), axis=0, tiled=True),
        model_index * half_width,
        half_width,
        1,
    )
    logit_terms = jnp.dot(halves, head_weight, preferred_element_type=jnp.float32)
    logits = lax.psum_scatter(logit_terms, "mp", scatter_dimension=0, tiled=True)
    local_ids = targets - vocab_index * logits.shape[1]
    columns = lax.broadcasted_iota(jnp.int32, logits.shape, 1)
    chosen = jnp.sum(jnp.where(columns == local_ids[:, None], logits, 0.0), axis=1)
    row_top = jnp.max(logits, axis=1)
    exp_total = jnp.sum(jnp.exp(logits - row_top[:, None]), axis=1)
    merged = merged_2((row_top, exp_total, chosen), "vocab", merge_stats)
    return merged[2] - merged[0] - jnp.log(merged[1])


def solution(mesh):
    return jax.shard_map(
        body,
        mesh=mesh,
        in_specs=(
            P(("groups", "vocab"), "mp"),
            P(("groups", "vocab"), "mp"),
            P("vocab", "mp"),
            P(("groups", "vocab", "mp"), None),
            P(),
            P("mp", "vocab"),
            P(("groups", "mp")),
        ),
        out_specs=P(("groups", "mp")),
        check_vma=False,
    )
```

profile of v0, /device:TPU:0, one launch (start us, length us, event | category | flops | bytes accessed | tf_op | source)
XLA Modules:
  0.0 128.8 jit_solution(11626139243467973319)
XLA Ops:
  6.5 0.0 copy-start.3
  6.5 0.0 copy-start.1
  6.5 0.0 copy-start
  6.5 0.0 copy-start.2
  6.5 0.9 fusion.12
  7.4 32.5 %all-gather.3 = bf16[8,2,7168]{2,1,0:T(2,128)(2,1)S(1)} all-gather(bf16[1,2,7168]{2,1,0:T(2,128)(2,1)S(1)} %fusion.12), channel_id=1, replica_groups=mesh['groups'=2,'vocab'=8,'mp'=2] {'vocab'}, dimensions={0}, use_global_device_ids=true | all-gather | bytes 258048 | tf_op jit(solution)/shard_map/all_gather | solution.py:36
  39.9 0.1 reshape.39
  40.0 9.1 %fusion.14 = f32[16,1024]{1,0:T(8,128)S(1)} fusion(bf16[16,7168]{1,0:T(8,128)(2,1)S(1)} %reshape.39, bf16[1024,7168]{1,0:T(8,128)(2,1)} %param.11), kind=kOutput, calls=%fused_computation.28 | convolution fusion | flops 234881024 | bytes 14974976 | tf_op jit(solution)/shard_map/dot_general | solution.py:35
  49.1 0.7 reshape.18
  49.7 5.5 %all-to-all-start = ((f32[8,2,1,1024]{3,1,2,0:T(2,128)}), f32[8,2,1,1024]{3,1,2,0:T(2,128)S(1)}, u32[]{:S(2)}, u32[]{:S(2)}) async-start(f32[8,2,1,1024]{3,1,2,0:T(2,128)} %bitcast.4), calls=%async_computation | async-start | bytes 131072 | tf_op jit(solution)/shard_map/all_to_all | solution.py:45
  55.2 0.0 reduce-scatter.2.cloned.1.call-start
  55.3 0.0 copy-done.1
  55.3 6.8 %all-to-all-done = f32[8,2,1,1024]{3,1,2,0:T(2,128)S(1)} async-done(((f32[8,2,1,1024]{3,1,2,0:T(2,128)}), f32[8,2,1,1024]{3,1,2,0:T(2,128)S(1)}, u32[]{:S(2)}, u32[]{:S(2)}) %all-to-all-start) | async-done | bytes 65568 | tf_op jit(solution)/shard_map/all_to_all | solution.py:45
  62.2 0.1 copy.10
  62.2 3.8 %all_to_all.27 = f32[1,2,1,8192]{3,2,0,1:T(1,128)S(1)} all-to-all(f32[1,2,1,8192]{3,2,0,1:T(1,128)S(1)} %copy.10), channel_id=1, replica_groups=mesh['groups'=2,'vocab'=8,'mp'=2] {'mp'}, dimensions={1} | all-to-all | bytes 131072 | tf_op jit(solution)/shard_map/all_to_all | solution.py:44
  66.0 0.1 reduce_sum.38
  66.1 0.0 copy-done
  66.2 0.7 multiply_reduce_fusion
  67.5 0.1 convert_bitcast_fusion
  67.6 19.5 %all-gather.4 = bf16[16,1,8192]{2,1,0:T(2,128)(2,1)S(1)} all-gather(bf16[1,1,8192]{2,1,0:T(2,128)(2,1)S(1)} %convert_bitcast_fusion), channel_id=1, replica_groups=mesh['groups'=2,'vocab'=8,'mp'=2] {'vocab','mp'}, dimensions={0}, use_global_device_ids=true | all-gather | bytes 278528 | tf_op jit(solution)/shard_map/all_gather | solution.py:61
  87.0 0.3 constant_dynamic-slice_fusion.3
  87.3 4.0 %fusion.7 = f32[16,504]{1,0:T(8,128)} fusion(bf16[4096,504]{0,1:T(8,128)(2,1)} %param.14, bf16[16,1,4096]{2,1,0:T(2,128)(2,1)S(1)} %constant_dynamic-slice_fusion.3), kind=kOutput, calls=%fused_computation.11 | convolution fusion | flops 66060288 | bytes 4292096 | tf_op jit(solution)/shard_map/dot_general | solution.py:66
  91.3 0.0 reduce-scatter.2.cloned.1.call-update
  91.3 0.0 copy-done.2
  91.4 0.0 copy-done.3
  91.4 0.6 dynamic-slice
  92.7 4.2 %reduce-scatter.2.cloned.1.call-done = f32[8,504]{1,0:T(8,128)} async-done(((f32[16,504]{1,0:T(8,128)}), f32[8,504]{1,0:T(8,128)}) %reduce-scatter.2.cloned.1.call-update) | async-done | bytes 16144 | tf_op jit(solution)/shard_map/reduce_scatter | solution.py:67
  96.8 0.8 reduce_max.9
  97.7 0.2 dynamic-update-slice
  97.9 0.9 select_reduce_fusion
  98.9 0.2 dynamic-update-slice.2
  99.1 0.2 dynamic-update-slice.1
  99.3 21.5 %all-reduce.3 = (f32[64]{0:T(128)S(1)}, f32[64]{0:T(128)S(1)}, f32[64]{0:T(128)S(1)}) all-reduce(f32[64]{0:T(128)S(1)} %dynamic-update-slice, f32[64]{0:T(128)S(1)} %dynamic-update-slice.1, f32[64]{0:T(128)S(1)} %dynamic-update-slice.2), channel_id=2, replica_groups=mesh['groups'=2,'vocab'=8,'mp'=2] {'vocab'}, use_global_device_ids=true, to_apply=%add | all-reduce | flops 192 | bytes 1536
  120.9 0.1 reshape.20
  120.9 0.1 reshape.21
  121.0 0.1 reshape.22
  121.1 0.3 while.19
  121.4 0.5 log_subtract_fusion
  (13 shorter events, 0.3 us)
Async XLA Ops:
  6.5 84.8 %copy-start.3 = (u32[32]{0:T(128)S(1)}, u32[32]{0:T(128)}, u32[]{:S(2)}) copy-start(u32[32]{0:T(128)} %constant.71) | copy-start | bytes 388
  6.5 48.8 %copy-start.1 = (bf16[8192]{0:T(1024)(128)(2,1)S(1)}, bf16[8192]{0:T(1024)(128)(2,1)}, u32[]{:S(2)}) copy-start(bf16[8192]{0:T(1024)(128)(2,1)} %param.13) | copy-start | bytes 49156
  6.5 59.6 %copy-start = (bf16[1,8192]{1,0:T(2,128)(2,1)S(1)}, bf16[1,8192]{1,0:T(2,128)(2,1)}, u32[]{:S(2)}) copy-start(bf16[1,8192]{1,0:T(2,128)(2,1)} %param.12) | copy-start | bytes 49156
  6.5 84.8 %copy-start.2 = (s32[8]{0:T(128)S(1)}, s32[8]{0:T(128)}, u32[]{:S(2)}) copy-start(s32[8]{0:T(128)} %param.15) | copy-start | bytes 100
  49.7 12.4 %all-to-all-start = ((f32[8,2,1,1024]{3,1,2,0:T(2,128)}), f32[8,2,1,1024]{3,1,2,0:T(2,128)S(1)}, u32[]{:S(2)}, u32[]{:S(2)}) async-start(f32[8,2,1,1024]{3,1,2,0:T(2,128)} %bitcast.4), calls=%async_computation | async-start | bytes 131072 | tf_op jit(solution)/shard_map/all_to_all | solution.py:45
  55.2 41.6 %reduce-scatter.2.cloned.1.call-start = ((), (), s32[]{:S(2)}) async-start(), calls=%async_computation.3 | async-start | bytes 49152 | tf_op jit(solution)/shard_map/reduce_scatter | solution.py:67
Sparse Core Ops, SparseCore 0:
  91.4 5.3 reduce-scatter.1
where the time goes:
time: 129 us
  blocking collectives  77.3 us (60%)
  between operations  14.9 us (12%)
  matrix products  13 us (10%)
  waiting for transfers between devices  11 us (9%)
  starting transfers between devices  5.54 us (4%)
  other arithmetic  4.22 us (3%)
  local copies, waits for them, and re-layouts  2.68 us (2%)
    all_gather x1, blocking collectives, body(): lax.all_gather(gated_units, 'vocab', axis=0, tiled=True)  32.5 us
    unnamed x1, blocking collectives  21.5 us
    all_gather x1, blocking collectives, body(): lax.all_gather(normed, ('vocab', 'mp'), axis=0, tiled=True)  19.5 us
    dot_general x1, matrix products, body(): lax.dot_general(lax.all_gather(gated_units, 'vocab', axis=0, tiled=True),...  9.05 us
    all_to_all x1, waiting for transfers between devices, body(): lax.all_to_all(grouped, 'vocab', split_axis=0, concat_axis=3, tiled=True)  6.83 us
    all_to_all x1, starting transfers between devices, body(): lax.all_to_all(grouped, 'vocab', split_axis=0, concat_axis=3, tiled=True)  5.51 us
    reduce_scatter x1, waiting for transfers between devices, body(): lax.psum_scatter(logit_terms, 'mp', scatter_dimension=0, tiled=True)  4.19 us
    dot_general x1, matrix products, body(): jnp.dot(halves, head_weight, preferred_element_type=jnp.float32)  3.98 us
  transfers between devices with their start and end apart: 2, of which 2 were waited for; matrix products, arithmetic and copies ran while one was open for 1% of the time, Pallas kernels for 0%

commit v1 on v0

--- a/solution.py
+++ b/solution.py
@@ -4,6 +4,18 @@
 from jax.sharding import PartitionSpec as P
 
 EPSILON = 1e-05
+
+
+def doubled_up(x, axis, dim):
+    ways, here, lap = (lax.axis_size(axis), lax.axis_index(axis), x.shape[dim])
+    line, have = (x, 1)
+    while have < ways:
+        line = jnp.concatenate(
+            [line, lax.ppermute(line, axis, [(d, (d - have) % ways) for d in range(ways)])],
+            axis=dim,
+        )
+        have = 2 * have
+    return jnp.roll(line, here * lap, axis=dim)
 
 
 def merged_2(value, axis, combine):
@@ -33,7 +45,7 @@
         jnp.bfloat16
     )
     down_terms = lax.dot_general(
-        lax.all_gather(gated_units, "vocab", axis=0, tiled=True),
+        doubled_up(gated_units, "vocab", 0),
         down_weight,
         (((1,), (1,)), ((), ())),
         preferred_element_type=jnp.float32,

time: 129 us -> 118 us (0.915)
  blocking collectives: 77.3 us -> 44.8 us
  waiting for transfers between devices: 11 us -> 21.9 us
  starting transfers between devices: 5.54 us -> 15.4 us
    all_gather x1 -> x0, blocking collectives: 32.5 us -> none  [body(): lax.all_gather(gated_units, 'vocab', axis=0, tiled=True)]
    ppermute x0 -> x3, waiting for transfers between devices: none -> 10.9 us  [doubled_up(): lax.ppermute(line, axis, [(d, (d - have) % ways) for d in range(ways)])]
    ppermute x0 -> x3, starting transfers between devices: none -> 7.93 us  [doubled_up(): lax.ppermute(line, axis, [(d, (d - have) % ways) for d in range(ways)])]
    all_to_all x1, starting transfers between devices: 5.51 us -> 7.47 us  [body(): lax.all_to_all(grouped, 'vocab', split_axis=0, concat_axis=3, tiled=True)]
  transfers between devices with their start and end apart: 2 -> 5, of which waited for: 2 -> 5; matrix products, arithmetic and copies ran while one was open for 1% -> 1% of each run, Pallas kernels for 0% -> 0%
where the time goes in v1:
time: 118 us; the launch traced here: 117 us
  blocking collectives  44.8 us (38%)
  waiting for transfers between devices  21.9 us (19%)
  starting transfers between devices  15.4 us (13%)
  between operations  14.9 us (13%)
  matrix products  13 us (11%)
  other arithmetic  4.39 us (4%)
  local copies, waits for them, and re-layouts  2.85 us (2%)
    unnamed x1, blocking collectives  21.5 us
    all_gather x1, blocking collectives, body(): lax.all_gather(normed, ('vocab', 'mp'), axis=0, tiled=True)  19.5 us
    ppermute x3, waiting for transfers between devices, doubled_up(): lax.ppermute(line, axis, [(d, (d - have) % ways) for d in range(ways)])  10.9 us
    dot_general x1, matrix products, body(): lax.dot_general(doubled_up(gated_units, 'vocab', 0), down_weight, (((1,),...  9.06 us
    ppermute x3, starting transfers between devices, doubled_up(): lax.ppermute(line, axis, [(d, (d - have) % ways) for d in range(ways)])  7.93 us
    all_to_all x1, starting transfers between devices, body(): lax.all_to_all(grouped, 'vocab', split_axis=0, concat_axis=3, tiled=True)  7.47 us
    all_to_all x1, waiting for transfers between devices, body(): lax.all_to_all(grouped, 'vocab', split_axis=0, concat_axis=3, tiled=True)  6.83 us
    reduce_scatter x1, waiting for transfers between devices, body(): lax.psum_scatter(logit_terms, 'mp', scatter_dimension=0, tiled=True)  4.19 us
  transfers between devices with their start and end apart: 5, of which 5 were waited for; matrix products, arithmetic and copies ran while one was open for 1% of the time, Pallas kernels for 0%

profile of v1, /device:TPU:0, one launch (start us, length us, event | category | flops | bytes accessed | tf_op | source)
XLA Modules:
  0.0 117.4 jit_solution(11887827784243195205)
XLA Ops:
  6.5 0.0 copy-start.3
  6.5 0.0 copy-start.1
  6.5 0.0 copy-start
  6.5 0.0 copy-start.2
  6.5 0.9 fusion.13
  7.4 6.1 %collective-permute-start = (bf16[2,7168]{1,0:T(2,128)(2,1)S(1)}, bf16[2,7168]{1,0:T(2,128)(2,1)S(1)}, u32[]{:S(2)}, u32[]{:S(2)}) collective-permute-start(bf16[2,7168]{1,0:T(2,128)(2,1)S(1)} %fusion.13), channel_id=1, source_target_pairs={{0,14},{2,0},{4,2},{6,4},{8,6},{10,8},{12,10},{14,12},{1,15},{3,1}... | collective-permute-start | bytes 86024 | tf_op jit(solution)/shard_map/ppermute | solution.py:14
  13.5 1.6 %collective-permute-done = bf16[2,7168]{1,0:T(2,128)(2,1)S(1)} collective-permute-done((bf16[2,7168]{1,0:T(2,128)(2,1)S(1)}, bf16[2,7168]{1,0:T(2,128)(2,1)S(1)}, u32[]{:S(2)}, u32[]{:S(2)}) %collective-permute-start) | collective-permute-done | bytes 28704 | tf_op jit(solution)/shard_map/ppermute | solution.py:14
  15.0 0.1 pad_maximum_fusion.1
  15.1 1.4 %collective-permute-start.1 = (bf16[4,7168]{1,0:T(4,128)(2,1)S(1)}, bf16[4,7168]{1,0:T(4,128)(2,1)S(1)}, u32[]{:S(2)}, u32[]{:S(2)}) collective-permute-start(bf16[4,7168]{1,0:T(4,128)(2,1)S(1)} %pad_maximum_fusion.1), channel_id=1, source_target_pairs={{0,12},{2,14},{4,0},{6,2},{8,4},{10,6},{12,8},{14,10},{1,13},{3,15... | collective-permute-start | bytes 172040 | tf_op jit(solution)/shard_map/ppermute | solution.py:14
  16.5 2.8 %collective-permute-done.1 = bf16[4,7168]{1,0:T(4,128)(2,1)S(1)} collective-permute-done((bf16[4,7168]{1,0:T(4,128)(2,1)S(1)}, bf16[4,7168]{1,0:T(4,128)(2,1)S(1)}, u32[]{:S(2)}, u32[]{:S(2)}) %collective-permute-start.1) | collective-permute-done | bytes 57376 | tf_op jit(solution)/shard_map/ppermute | solution.py:14
  19.3 0.1 pad_maximum_fusion
  19.4 0.4 collective-permute-start.2
  19.9 6.5 %collective-permute-done.2 = bf16[8,7168]{1,0:T(8,128)(2,1)S(1)} collective-permute-done((bf16[8,7168]{1,0:T(8,128)(2,1)S(1)}, bf16[8,7168]{1,0:T(8,128)(2,1)S(1)}, u32[]{:S(2)}, u32[]{:S(2)}) %collective-permute-start.2) | collective-permute-done | bytes 114720 | tf_op jit(solution)/shard_map/ppermute | solution.py:14
  26.4 0.3 concatenate.16
  26.7 9.1 %fusion.7 = f32[16,1024]{1,0:T(8,128)S(1)} fusion(bf16[1024,7168]{1,0:T(8,128)(2,1)} %param.11, bf16[32,7168]{1,0:T(8,128)(2,1)S(1)} %concatenate.16, s32[]{:T(128)S(6)} %select_n.33), kind=kOutput, calls=%fused_computation.10 | convolution fusion | flops 234881024 | bytes 14974980 | tf_op jit(solution)/shard_map/dot_general | solution.py:47
  35.7 0.7 reshape.18
  36.4 7.5 %all-to-all-start = ((f32[8,2,1,1024]{3,1,2,0:T(2,128)}), f32[8,2,1,1024]{3,1,2,0:T(2,128)S(1)}, u32[]{:S(2)}, u32[]{:S(2)}) async-start(f32[8,2,1,1024]{3,1,2,0:T(2,128)} %bitcast.3), calls=%async_computation | async-start | bytes 131072 | tf_op jit(solution)/shard_map/all_to_all | solution.py:57
  43.9 0.0 reduce-scatter.2.cloned.1.call-start
  43.9 0.0 copy-done.1
  44.0 6.8 %all-to-all-done = f32[8,2,1,1024]{3,1,2,0:T(2,128)S(1)} async-done(((f32[8,2,1,1024]{3,1,2,0:T(2,128)}), f32[8,2,1,1024]{3,1,2,0:T(2,128)S(1)}, u32[]{:S(2)}, u32[]{:S(2)}) %all-to-all-start) | async-done | bytes 65568 | tf_op jit(solution)/shard_map/all_to_all | solution.py:57
  50.8 0.1 copy.10
  50.9 3.8 %all_to_all.27 = f32[1,2,1,8192]{3,2,0,1:T(1,128)S(1)} all-to-all(f32[1,2,1,8192]{3,2,0,1:T(1,128)S(1)} %copy.10), channel_id=1, replica_groups=mesh['groups'=2,'vocab'=8,'mp'=2] {'mp'}, dimensions={1} | all-to-all | bytes 131072 | tf_op jit(solution)/shard_map/all_to_all | solution.py:56
  54.7 0.1 reduce_sum.38
  54.7 0.0 copy-done
  54.8 0.7 multiply_reduce_fusion
  56.2 0.1 convert_bitcast_fusion
  56.2 19.5 %all-gather.3 = bf16[16,1,8192]{2,1,0:T(2,128)(2,1)S(1)} all-gather(bf16[1,1,8192]{2,1,0:T(2,128)(2,1)S(1)} %convert_bitcast_fusion), channel_id=1, replica_groups=mesh['groups'=2,'vocab'=8,'mp'=2] {'vocab','mp'}, dimensions={0}, use_global_device_ids=true | all-gather | bytes 278528 | tf_op jit(solution)/shard_map/all_gather | solution.py:73
  75.7 0.3 constant_dynamic-slice_fusion.3
  76.0 4.0 %fusion.9 = f32[16,504]{1,0:T(8,128)} fusion(bf16[4096,504]{0,1:T(8,128)(2,1)} %param.14, bf16[16,1,4096]{2,1,0:T(2,128)(2,1)S(1)} %constant_dynamic-slice_fusion.3), kind=kOutput, calls=%fused_computation.13 | convolution fusion | flops 66060288 | bytes 4292096 | tf_op jit(solution)/shard_map/dot_general | solution.py:78
  79.9 0.0 reduce-scatter.2.cloned.1.call-update
  80.0 0.0 copy-done.2
  80.0 0.0 copy-done.3
  80.0 0.6 dynamic-slice
  81.3 4.2 %reduce-scatter.2.cloned.1.call-done = f32[8,504]{1,0:T(8,128)} async-done(((f32[16,504]{1,0:T(8,128)}), f32[8,504]{1,0:T(8,128)}) %reduce-scatter.2.cloned.1.call-update) | async-done | bytes 16144 | tf_op jit(solution)/shard_map/reduce_scatter | solution.py:79
  85.5 0.8 reduce_max.9
  86.3 0.2 dynamic-update-slice
  86.6 0.9 select_reduce_fusion
  87.5 0.2 dynamic-update-slice.2
  87.7 0.2 dynamic-update-slice.1
  88.0 21.5 %all-reduce.3 = (f32[64]{0:T(128)S(1)}, f32[64]{0:T(128)S(1)}, f32[64]{0:T(128)S(1)}) all-reduce(f32[64]{0:T(128)S(1)} %dynamic-update-slice, f32[64]{0:T(128)S(1)} %dynamic-update-slice.1, f32[64]{0:T(128)S(1)} %dynamic-update-slice.2), channel_id=2, replica_groups=mesh['groups'=2,'vocab'=8,'mp'=2] {'vocab'}, use_global_device_ids=true, to_apply=%add | all-reduce | flops 192 | bytes 1536
  109.5 0.1 reshape.20
  109.6 0.1 reshape.21
  109.6 0.1 reshape.22
  109.7 0.3 while.19
  110.0 0.5 log_subtract_fusion
  (13 shorter events, 0.3 us)
Async XLA Ops:
  6.5 73.5 %copy-start.3 = (u32[32]{0:T(128)S(1)}, u32[32]{0:T(128)}, u32[]{:S(2)}) copy-start(u32[32]{0:T(128)} %constant.94) | copy-start | bytes 388
  6.5 37.4 %copy-start.1 = (bf16[8192]{0:T(1024)(128)(2,1)S(1)}, bf16[8192]{0:T(1024)(128)(2,1)}, u32[]{:S(2)}) copy-start(bf16[8192]{0:T(1024)(128)(2,1)} %param.13) | copy-start | bytes 49156
  6.5 48.2 %copy-start = (bf16[1,8192]{1,0:T(2,128)(2,1)S(1)}, bf16[1,8192]{1,0:T(2,128)(2,1)}, u32[]{:S(2)}) copy-start(bf16[1,8192]{1,0:T(2,128)(2,1)} %param.12) | copy-start | bytes 49156
  6.5 73.4 %copy-start.2 = (s32[8]{0:T(128)S(1)}, s32[8]{0:T(128)}, u32[]{:S(2)}) copy-start(s32[8]{0:T(128)} %param.15) | copy-start | bytes 100
  7.4 7.6 %collective-permute-start = (bf16[2,7168]{1,0:T(2,128)(2,1)S(1)}, bf16[2,7168]{1,0:T(2,128)(2,1)S(1)}, u32[]{:S(2)}, u32[]{:S(2)}) collective-permute-start(bf16[2,7168]{1,0:T(2,128)(2,1)S(1)} %fusion.13), channel_id=1, source_target_pairs={{0,14},{2,0},{4,2},{6,4},{8,6},{10,8},{12,10},{14,12},{1,15},{3,1}... | collective-permute-start | bytes 86024 | tf_op jit(solution)/shard_map/ppermute | solution.py:14
  15.1 4.2 %collective-permute-start.1 = (bf16[4,7168]{1,0:T(4,128)(2,1)S(1)}, bf16[4,7168]{1,0:T(4,128)(2,1)S(1)}, u32[]{:S(2)}, u32[]{:S(2)}) collective-permute-start(bf16[4,7168]{1,0:T(4,128)(2,1)S(1)} %pad_maximum_fusion.1), channel_id=1, source_target_pairs={{0,12},{2,14},{4,0},{6,2},{8,4},{10,6},{12,8},{14,10},{1,13},{3,15... | collective-permute-start | bytes 172040 | tf_op jit(solution)/shard_map/ppermute | solution.py:14
  19.4 7.0 %collective-permute-start.2 = (bf16[8,7168]{1,0:T(8,128)(2,1)S(1)}, bf16[8,7168]{1,0:T(8,128)(2,1)S(1)}, u32[]{:S(2)}, u32[]{:S(2)}) collective-permute-start(bf16[8,7168]{1,0:T(8,128)(2,1)S(1)} %pad_maximum_fusion), channel_id=1, source_target_pairs={{0,8},{2,10},{4,12},{6,14},{8,0},{10,2},{12,4},{14,6},{1,9},{3,11}... | collective-permute-start | bytes 344072 | tf_op jit(solution)/shard_map/ppermute | solution.py:14
  36.4 14.4 %all-to-all-start = ((f32[8,2,1,1024]{3,1,2,0:T(2,128)}), f32[8,2,1,1024]{3,1,2,0:T(2,128)S(1)}, u32[]{:S(2)}, u32[]{:S(2)}) async-start(f32[8,2,1,1024]{3,1,2,0:T(2,128)} %bitcast.3), calls=%async_computation | async-start | bytes 131072 | tf_op jit(solution)/shard_map/all_to_all | solution.py:57
  43.9 41.6 %reduce-scatter.2.cloned.1.call-start = ((), (), s32[]{:S(2)}) async-start(), calls=%async_computation.3 | async-start | bytes 49152 | tf_op jit(solution)/shard_map/reduce_scatter | solution.py:79
Sparse Core Ops, SparseCore 0:
  80.1 5.3 reduce-scatter.1
